TPU v7x, 256 devices: a whole 4x4x8 slice. The times are simulated.
256 devices in a mesh: fsdp: 16 (over y, x), ep: 16 (over z, core).
Axes of the slice: x: 4, y: 4, z: 8, core: 2. Of those that a mesh axis runs over, the one named last changes fastest.
Arguments:
- tokens: bfloat16 [8192, 7168], P('ep', 'fsdp'), may hold values from -6 to 6
- cotangent: bfloat16 [8192, 7168], P('ep', 'fsdp'), may hold values from -3 to 3
- gate_weight: bfloat16 [16, 7168, 2048], P('ep', None, 'fsdp'), may hold values from -0.0625 to 0.0625
- up_weight: bfloat16 [16, 7168, 2048], P('ep', None, 'fsdp'), may hold values from -0.0625 to 0.0625
- down_weight: bfloat16 [16, 2048, 7168], P('ep', 'fsdp'), may hold values from -0.125 to 0.125
- chosen: int32 [16, 16, 16], P(None, 'ep'), may hold values from 0 to 511, as said below
- counts: int32 [16, 16], P(None, 'ep'), may hold values from 1 to 16, as said below
- gate_prob: float32 [16, 16, 16], P(None, 'ep'), may hold values from 0.2 to 1
Outputs:
- mixture: bfloat16 [8192, 7168], P('ep', 'fsdp')
- grad_tokens: bfloat16 [8192, 7168], P('ep', 'fsdp')
- grad_gate: bfloat16 [16, 7168, 2048], P('ep', None, 'fsdp')
- grad_up: bfloat16 [16, 7168, 2048], P('ep', None, 'fsdp')
- grad_down: bfloat16 [16, 2048, 7168], P('ep', 'fsdp')
Inputs may be any that keep to these rules, and one draw needn't show every extreme that they name: For each expert e and group s the entries chosen[e, s, j] with j < counts[e, s] are distinct; the remaining entries are padding. `counts`: in every draw one expert takes 16 rows from every group.
All inputs are finite; a program needn't handle non-finite values.
Results may differ from a plain program's by a relative error of at most 0.017.
Values may be sent and summed in bfloat16 or wider, within the bound.
A program may use at most 192 MiB of HBM per device.

v0:
```python
import jax
import jax.numpy as jnp
from jax import lax
from jax.sharding import PartitionSpec as P


def pick_rows(tokens, cotangent, row_index, live_mask, weight):
    flat_rows = row_index.reshape(-1)
    keep_rows = live_mask.reshape(-1)[:, None]
    taken_tokens = jnp.take(tokens, flat_rows, axis=0)
    picked_tokens = jnp.where(keep_rows, taken_tokens, jnp.zeros_like(taken_tokens))
    taken_grads = jnp.take(cotangent, flat_rows, axis=0).astype(jnp.float32)
    picked_grads = (weight.reshape(-1)[:, None] * taken_grads).astype(jnp.bfloat16)
    shaped = row_index.shape + (tokens.shape[1],)
    return (picked_tokens.reshape(shaped), picked_grads.reshape(shaped))


def to_slots(summed, experts, slot_count):
    return summed.astype(jnp.bfloat16).reshape(experts, slot_count, summed.shape[1])


def send_back(term, experts, slot_count):
    summed = lax.psum_scatter(
        term.astype(jnp.bfloat16), "fsdp", scatter_dimension=1, tiled=True
    ).astype(jnp.float32)
    return lax.all_to_all(
        to_slots(summed, experts, slot_count), "ep", split_axis=0, concat_axis=0, tiled=True
    )


def per_device(tokens, cotangent, gate_weight, up_weight, down_weight, chosen, counts, gate_prob):
    experts = chosen.shape[0]
    slot_count = chosen.shape[2]
    features = tokens.shape[1]
    row_index = chosen[:, 0, :]
    position = lax.broadcasted_iota(jnp.int32, (experts, slot_count), 1)
    live_mask = position < counts
    weight = jnp.where(live_mask, gate_prob[:, 0, :], 0.0)
    picked_tokens, picked_grads = pick_rows(tokens, cotangent, row_index, live_mask, weight)
    wide_tokens, wide_grads = (
        lax.all_gather(picked_tokens, "fsdp", axis=2, tiled=True),
        lax.all_gather(picked_grads, "fsdp", axis=2, tiled=True),
    )
    rows_tokens, rows_grads = (
        lax.all_to_all(wide_tokens, "ep", split_axis=0, concat_axis=0, tiled=True),
        lax.all_to_all(wide_grads, "ep", split_axis=0, concat_axis=0, tiled=True),
    )
    full_width = rows_tokens.shape[2]
    total_rows = rows_tokens.shape[0] * slot_count
    rows_tokens = rows_tokens.reshape(total_rows, full_width)
    rows_grads = rows_grads.reshape(total_rows, full_width)
    gate_local = gate_weight[0]
    up_local = up_weight[0]
    down_local = down_weight[0]
    pre_gate = jnp.dot(rows_tokens, gate_local, preferred_element_type=jnp.float32)
    pre_up = jnp.dot(rows_tokens, up_local, preferred_element_type=jnp.float32)
    sigmoid_gate = jax.nn.sigmoid(pre_gate)
    activated = pre_gate * sigmoid_gate
    hidden = (activated * pre_up).astype(jnp.bfloat16)
    output_term = jnp.dot(hidden, down_local, preferred_element_type=jnp.float32)
    output_back = send_back(output_term, experts, slot_count)
    contract_rows = (((0,), (0,)), ((), ()))
    contract_last = (((1,), (1,)), ((), ()))
    grad_hidden = lax.dot_general(
        rows_grads, down_local, contract_last, preferred_element_type=jnp.float32
    )
    grad_pre_gate = (
        grad_hidden * pre_up * sigmoid_gate * (1.0 + pre_gate * (1.0 - sigmoid_gate))
    ).astype(jnp.bfloat16)
    grad_pre_up = (grad_hidden * activated).astype(jnp.bfloat16)
    grad_down = lax.dot_general(
        hidden, rows_grads, contract_rows, preferred_element_type=jnp.float32
    ).astype(jnp.bfloat16)
    grad_gate = lax.dot_general(
        rows_tokens, grad_pre_gate, contract_rows, preferred_element_type=jnp.float32
    ).astype(jnp.bfloat16)
    grad_up = lax.dot_general(
        rows_tokens, grad_pre_up, contract_rows, preferred_element_type=jnp.float32
    ).astype(jnp.bfloat16)
    grad_term = lax.dot_general(
        grad_pre_gate, gate_local, contract_last, preferred_element_type=jnp.float32
    )
    grad_term = grad_term + lax.dot_general(
        grad_pre_up, up_local, contract_last, preferred_element_type=jnp.float32
    )
    grad_back = send_back(grad_term, experts, slot_count)
    flat_rows = row_index.reshape(-1)
    output_rows = output_back.reshape(-1, features).astype(jnp.float32)
    mixture = (
        jnp.zeros((tokens.shape[0], features), jnp.float32)
        .at[flat_rows]
        .add(weight.reshape(-1)[:, None] * output_rows)
    )
    grad_rows = jnp.where(
        live_mask.reshape(-1)[:, None], grad_back.reshape(-1, features).astype(jnp.float32), 0.0
    )
    grad_tokens = jnp.zeros((tokens.shape[0], features), jnp.float32).at[flat_rows].add(grad_rows)
    return (
        mixture.astype(jnp.bfloat16),
        grad_tokens.astype(jnp.bfloat16),
        grad_gate[None],
        grad_up[None],
        grad_down[None],
    )


def solution(mesh):
    placed = (
        P("ep", "fsdp"),
        P("ep", "fsdp"),
        P("ep", None, "fsdp"),
        P("ep", None, "fsdp"),
        P("ep", "fsdp", None),
        P(None, "ep", None),
        P(None, "ep"),
        P(None, "ep", None),
    )
    return jax.shard_map(
        per_device,
        mesh=mesh,
        in_specs=placed,
        out_specs=(
            P("ep", "fsdp"),
            P("ep", "fsdp"),
            P("ep", None, "fsdp"),
            P("ep", None, "fsdp"),
            P("ep", "fsdp", None),
        ),
        check_vma=False,
    )
```

profile of v0, /device:TPU:1, one launch (start us, length us, event | category | flops | bytes accessed | tf_op | source)
XLA Modules:
  0.0 701.6 jit_solution(7673215205043818833)
XLA Ops:
  11.5 1.9 copy.32
  16.3 1.9 copy.36
  18.3 179.5 %all-gather.3.cloned.1.call-done = bf16[16,16,7168]{1,0,2:T(8,128)(2,1)} async-done(((bf16[16,16,448]{1,0,2:T(8,128)(2,1)}), bf16[16,16,7168]{1,0,2:T(8,128)(2,1)}) %all-gather.3.cloned.1.call-update) | async-done | bytes 3670032 | tf_op jit(solution)/shard_map/all_gather | solution.py:41
  197.8 26.9 %copy.33 = bf16[16,16,7168]{2,1,0:T(8,128)(2,1)} copy(bf16[16,16,7168]{1,0,2:T(8,128)(2,1)} %all-gather.3.cloned.1.call-done) | data formatting | bytes 7340032 | tf_op jit(solution)/shard_map/all_gather | solution.py:41
  224.7 7.9 %all-to-all-start = ((bf16[16,16,7168]{2,1,0:T(8,128)(2,1)}), bf16[16,16,7168]{2,1,0:T(8,128)(2,1)}, u32[]{:S(2)}, u32[]{:S(2)}) async-start(bf16[16,16,7168]{2,1,0:T(8,128)(2,1)} %copy.33), calls=%async_computation | async-start | bytes 7340032 | tf_op jit(solution)/shard_map/all_to_all | solution.py:45
  232.6 148.5 %all-gather.5.cloned.1.call-done = bf16[16,16,7168]{1,0,2:T(8,128)(2,1)} async-done(((bf16[16,16,448]{1,0,2:T(8,128)(2,1)}), bf16[16,16,7168]{1,0,2:T(8,128)(2,1)}) %all-gather.5.cloned.1.call-update) | async-done | bytes 3670032 | tf_op jit(solution)/shard_map/all_gather | solution.py:42
  381.1 26.5 %copy.37 = bf16[16,16,7168]{2,1,0:T(8,128)(2,1)} copy(bf16[16,16,7168]{1,0,2:T(8,128)(2,1)} %all-gather.5.cloned.1.call-done) | data formatting | bytes 7340032 | tf_op jit(solution)/shard_map/all_gather | solution.py:42
  407.6 7.9 %all-to-all-start.2 = ((bf16[16,16,7168]{2,1,0:T(8,128)(2,1)}), bf16[16,16,7168]{2,1,0:T(8,128)(2,1)}, u32[]{:S(2)}, u32[]{:S(2)}) async-start(bf16[16,16,7168]{2,1,0:T(8,128)(2,1)} %copy.37), calls=%async_computation.3 | async-start | bytes 7340032 | tf_op jit(solution)/shard_map/all_to_all | solution.py:46
  415.5 3.8 fusion.8
  419.4 3.2 fusion.12
  422.6 75.2 %all-to-all-done.2 = bf16[16,16,7168]{2,1,0:T(8,128)(2,1)} async-done(((bf16[16,16,7168]{2,1,0:T(8,128)(2,1)}), bf16[16,16,7168]{2,1,0:T(8,128)(2,1)}, u32[]{:S(2)}, u32[]{:S(2)}) %all-to-all-start.2) | async-done | bytes 3670048 | tf_op jit(solution)/shard_map/all_to_all | solution.py:46
  497.7 3.2 multiply_convert_fusion.1
  500.9 3.1 convolution_convert_fusion
  504.1 2.7 fusion.10
  506.8 2.9 fusion
  511.2 71.2 %reduce-scatter.3.cloned.1.call-done = bf16[256,448]{0,1:T(8,128)(2,1)} async-done(((bf16[256,7168]{0,1:T(8,128)(2,1)}), bf16[256,448]{0,1:T(8,128)(2,1)}) %reduce-scatter.3.cloned.1.call-update) | async-done | bytes 229392 | tf_op jit(solution)/shard_map/reduce_scatter | solution.py:23
  584.2 9.4 %all-to-all-start.1 = ((bf16[16,16,448]{2,1,0:T(8,128)(2,1)}), bf16[16,16,448]{2,1,0:T(8,128)(2,1)S(1)}, u32[]{:S(2)}, u32[]{:S(2)}) async-start(bf16[16,16,448]{2,1,0:T(8,128)(2,1)} %bitcast.7), calls=%async_computation.2 | async-start | bytes 524288 | tf_op jit(solution)/shard_map/all_to_all | solution.py:26
  593.6 3.9 fusion.3
  597.5 70.1 %reduce-scatter.5.cloned.1.call-done = bf16[256,448]{0,1:T(8,128)(2,1)} async-done(((bf16[256,7168]{0,1:T(8,128)(2,1)}), bf16[256,448]{0,1:T(8,128)(2,1)}) %reduce-scatter.5.cloned.1.call-update) | async-done | bytes 229392 | tf_op jit(solution)/shard_map/reduce_scatter | solution.py:23
  669.4 9.4 %all-to-all-start.3 = ((bf16[16,16,448]{2,1,0:T(8,128)(2,1)}), bf16[16,16,448]{2,1,0:T(8,128)(2,1)}, u32[]{:S(2)}, u32[]{:S(2)}) async-start(bf16[16,16,448]{2,1,0:T(8,128)(2,1)} %bitcast.11), calls=%async_computation.5 | async-start | bytes 524288 | tf_op jit(solution)/shard_map/all_to_all | solution.py:26
  678.8 4.4 fusion.2
  683.2 4.4 fusion.1
  687.6 2.4 scatter_custom_fusion
  691.1 2.8 scatter_custom_fusion.1
  (49 shorter events, 14.3 us)
Async XLA Ops:
  7.2 490.6 %copy-start = (bf16[1,128,7168]{2,1,0:T(8,128)(2,1)S(1)}, bf16[1,128,7168]{2,1,0:T(8,128)(2,1)}, u32[]{:S(2)}) copy-start(bf16[1,128,7168]{2,1,0:T(8,128)(2,1)} %param.14) | copy-start | bytes 5505028
  7.2 190.6 %all-gather.3.cloned.1.call-start = ((), (), s32[]{:S(2)}) async-start(), calls=%async_computation.6 | async-start | bytes 31195136 | tf_op jit(solution)/shard_map/all_gather | solution.py:41
  9.0 5.1 copy-start.5
  10.2 4.6 copy-start.3
  13.5 367.6 %all-gather.5.cloned.1.call-start = ((), (), s32[]{:S(2)}) async-start(), calls=%async_computation.8 | async-start | bytes 31195136 | tf_op jit(solution)/shard_map/all_gather | solution.py:42
  224.7 182.9 %all-to-all-start = ((bf16[16,16,7168]{2,1,0:T(8,128)(2,1)}), bf16[16,16,7168]{2,1,0:T(8,128)(2,1)}, u32[]{:S(2)}, u32[]{:S(2)}) async-start(bf16[16,16,7168]{2,1,0:T(8,128)(2,1)} %copy.33), calls=%async_computation | async-start | bytes 7340032 | tf_op jit(solution)/shard_map/all_to_all | solution.py:45
  407.6 90.1 %all-to-all-start.2 = ((bf16[16,16,7168]{2,1,0:T(8,128)(2,1)}), bf16[16,16,7168]{2,1,0:T(8,128)(2,1)}, u32[]{:S(2)}, u32[]{:S(2)}) async-start(bf16[16,16,7168]{2,1,0:T(8,128)(2,1)} %copy.37), calls=%async_computation.3 | async-start | bytes 7340032 | tf_op jit(solution)/shard_map/all_to_all | solution.py:46
  415.5 166.9 %reduce-scatter.3.cloned.1.call-start = ((), (), s32[]{:S(2)}) async-start(), calls=%async_computation.7 | async-start | bytes 3899392 | tf_op jit(solution)/shard_map/reduce_scatter | solution.py:23
  415.5 3.9 copy-start.2
  504.0 163.6 %reduce-scatter.5.cloned.1.call-start = ((), (), s32[]{:S(2)}) async-start(), calls=%async_computation.9 | async-start | bytes 3899392 | tf_op jit(solution)/shard_map/reduce_scatter | solution.py:23
  504.1 2.8 copy-start.1
  509.8 0.7 copy-start.4
  584.2 85.2 %all-to-all-start.1 = ((bf16[16,16,448]{2,1,0:T(8,128)(2,1)}), bf16[16,16,448]{2,1,0:T(8,128)(2,1)S(1)}, u32[]{:S(2)}, u32[]{:S(2)}) async-start(bf16[16,16,448]{2,1,0:T(8,128)(2,1)} %bitcast.7), calls=%async_computation.2 | async-start | bytes 524288 | tf_op jit(solution)/shard_map/all_to_all | solution.py:26
  669.4 21.7 %all-to-all-start.3 = ((bf16[16,16,448]{2,1,0:T(8,128)(2,1)}), bf16[16,16,448]{2,1,0:T(8,128)(2,1)}, u32[]{:S(2)}, u32[]{:S(2)}) async-start(bf16[16,16,448]{2,1,0:T(8,128)(2,1)} %bitcast.11), calls=%async_computation.5 | async-start | bytes 524288 | tf_op jit(solution)/shard_map/all_to_all | solution.py:26
Sparse Core Ops, SparseCore 0:
  13.6 184.1 all-gather.2
  200.8 180.2 all-gather.4
  504.1 78.2 reduce-scatter.2
  585.9 81.6 reduce-scatter.4
where the time goes:
time: 704 us; the launch traced here: 702 us
  waiting for transfers between devices  545 us (77%)
  local copies, waits for them, and re-layouts  68.8 us (10%)
  starting transfers between devices  34.7 us (5%)
  matrix products  31.8 us (5%)
  between operations  13.9 us (2%)
  other arithmetic  7.78 us (1%)
    all_gather x1, waiting for transfers between devices, per_device(): lax.all_gather(picked_tokens, 'fsdp', axis=2, tiled=True)  180 us
    all_gather x1, waiting for transfers between devices, per_device(): lax.all_gather(picked_grads, 'fsdp', axis=2, tiled=True)  148 us
    reduce_scatter x2, waiting for transfers between devices, send_back(): lax.psum_scatter(term.astype(jnp.bfloat16), 'fsdp', scatter_dimension=1,...  141 us
    all_to_all x1, waiting for transfers between devices, per_device(): lax.all_to_all(wide_grads, 'ep', split_axis=0, concat_axis=0, tiled=True)  75.2 us
    all_gather x1, local copies, waits for them, and re-layouts, per_device(): lax.all_gather(picked_tokens, 'fsdp', axis=2, tiled=True)  26.9 us
    all_gather x1, local copies, waits for them, and re-layouts, per_device(): lax.all_gather(picked_grads, 'fsdp', axis=2, tiled=True)  26.5 us
    all_to_all x2, starting transfers between devices, send_back(): lax.all_to_all(to_slots(summed, experts, slot_count), 'ep', split_axis=0,...  18.8 us
  transfers between devices with their start and end apart: 8, of which 5 were waited for; matrix products, arithmetic and copies ran while one was open for 13% of the time, Pallas kernels for 0%

commit v1 on v0

--- a/solution.py
+++ b/solution.py
@@ -38,7 +38,9 @@
     weight = jnp.where(live_mask, gate_prob[:, 0, :], 0.0)
     picked_tokens, picked_grads = pick_rows(tokens, cotangent, row_index, live_mask, weight)
     wide_tokens, wide_grads = (
-        lax.all_gather(picked_tokens, "fsdp", axis=2, tiled=True),
+        jnp.concatenate(
+            lax.all_to_all(jnp.stack([picked_tokens] * lax.axis_size("fsdp")), "fsdp", 0, 0), axis=2
+        ),
         lax.all_gather(picked_grads, "fsdp", axis=2, tiled=True),
     )
     rows_tokens, rows_grads = (

time: 704 us -> 558 us (0.79)
  waiting for transfers between devices: 545 us -> 397 us
  starting transfers between devices: 34.7 us -> 48.6 us
  local copies, waits for them, and re-layouts: 68.8 us -> 57.6 us
    all_gather x1 -> x0, waiting for transfers between devices: 180 us -> none  [per_device(): lax.all_gather(picked_tokens, 'fsdp', axis=2, tiled=True)]
    all_to_all x0 -> x1, waiting for transfers between devices: none -> 65.6 us  [per_device(): lax.all_to_all(jnp.stack([picked_tokens] * lax.axis_size('fsdp')), 'fsdp'...]
    all_gather x1, waiting for transfers between devices: 148 us -> 115 us  [per_device(): lax.all_gather(picked_grads, 'fsdp', axis=2, tiled=True)]
    all_gather x1 -> x0, local copies, waits for them, and re-layouts: 26.9 us -> none  [per_device(): lax.all_gather(picked_tokens, 'fsdp', axis=2, tiled=True)]
    reshape x0 -> x2, local copies, waits for them, and re-layouts: none -> 15 us  [per_device(): jnp.concatenate(lax.all_to_all(jnp.stack([picked_tokens] * lax.axis_size(...]
    all_to_all x0 -> x1, starting transfers between devices: none -> 7.76 us  [per_device(): lax.all_to_all(jnp.stack([picked_tokens] * lax.axis_size('fsdp')), 'fsdp'...]
  transfers between devices with their start and end apart: 8 -> 8, of which waited for: 5 -> 5; matrix products, arithmetic and copies ran while one was open for 13% -> 14% of each run, Pallas kernels for 0% -> 0%
where the time goes in v1:
time: 558 us; the launch traced here: 557 us
  waiting for transfers between devices  397 us (71%)
  local copies, waits for them, and re-layouts  57.6 us (10%)
  starting transfers between devices  48.6 us (9%)
  matrix products  31.8 us (6%)
  between operations  13.9 us (2%)
  other arithmetic  7.78 us (1%)
    reduce_scatter x2, waiting for transfers between devices, send_back(): lax.psum_scatter(term.astype(jnp.bfloat16), 'fsdp', scatter_dimension=1,...  141 us
    all_gather x1, waiting for transfers between devices, per_device(): lax.all_gather(picked_grads, 'fsdp', axis=2, tiled=True)  115 us
    all_to_all x1, waiting for transfers between devices, per_device(): lax.all_to_all(wide_grads, 'ep', split_axis=0, concat_axis=0, tiled=True)  75 us
    all_to_all x1, waiting for transfers between devices, per_device(): lax.all_to_all(jnp.stack([picked_tokens] * lax.axis_size('fsdp')), 'fsdp'...  65.6 us
    all_gather x1, local copies, waits for them, and re-layouts, per_device(): lax.all_gather(picked_grads, 'fsdp', axis=2, tiled=True)  26.5 us
    all_to_all x2, starting transfers between devices, send_back(): lax.all_to_all(to_slots(summed, experts, slot_count), 'ep', split_axis=0,...  18.7 us
    reshape x2, local copies, waits for them, and re-layouts, per_device(): jnp.concatenate(lax.all_to_all(jnp.stack([picked_tokens] * lax.axis_size(...  15 us
    all_to_all x1, starting transfers between devices, per_device(): lax.all_to_all(wide_tokens, 'ep', split_axis=0, concat_axis=0, tiled=True)  13.9 us
  transfers between devices with their start and end apart: 8, of which 5 were waited for; matrix products, arithmetic and copies ran while one was open for 14% of the time, Pallas kernels for 0%

profile of v1, /device:TPU:1, one launch (start us, length us, event | category | flops | bytes accessed | tf_op | source)
XLA Modules:
  0.0 556.8 jit_solution(7177601298227461966)
XLA Ops:
  11.5 2.6 stack.3
  14.1 7.8 %all-to-all-start = ((bf16[16,16,16,448]{3,2,1,0:T(8,128)(2,1)}), bf16[16,16,16,448]{3,2,1,0:T(8,128)(2,1)}, u32[]{:S(2)}, u32[]{:S(2)}) async-start(bf16[16,16,16,448]{3,2,1,0:T(8,128)(2,1)} %stack.3), calls=%async_computation | async-start | bytes 8388608 | tf_op jit(solution)/shard_map/all_to_all | solution.py:42
  26.6 65.6 %all-to-all-done = bf16[16,16,16,448]{3,2,1,0:T(8,128)(2,1)} async-done(((bf16[16,16,16,448]{3,2,1,0:T(8,128)(2,1)}), bf16[16,16,16,448]{3,2,1,0:T(8,128)(2,1)}, u32[]{:S(2)}, u32[]{:S(2)}) %all-to-all-start) | async-done | bytes 3670048 | tf_op jit(solution)/shard_map/all_to_all | solution.py:42
  92.3 7.1 %copy.32 = bf16[16,16,16,448]{3,2,1,0:T(8,128)(2,1)} copy(bf16[16,16,16,448]{3,1,0,2:T(8,128)(2,1)} %bitcast.3) | data formatting | bytes 7340032 | tf_op jit(solution)/shard_map/reshape | solution.py:41
  99.3 7.9 %reshape.102 = bf16[16,16,7168]{2,1,0:T(8,128)(2,1)} reshape(bf16[16,16,16,448]{3,2,1,0:T(8,128)(2,1)} %copy.32) | data formatting | bytes 7340032 | tf_op jit(solution)/shard_map/reshape | solution.py:41
  107.3 13.9 %all-to-all-start.1 = ((bf16[16,16,7168]{2,1,0:T(8,128)(2,1)}), bf16[16,16,7168]{2,1,0:T(8,128)(2,1)}, u32[]{:S(2)}, u32[]{:S(2)}) async-start(bf16[16,16,7168]{2,1,0:T(8,128)(2,1)} %reshape.102), calls=%async_computation.1 | async-start | bytes 7340032 | tf_op jit(solution)/shard_map/all_to_all | solution.py:47
  121.2 115.2 %all-gather.2.cloned.1.call-done = bf16[16,16,7168]{1,0,2:T(8,128)(2,1)} async-done(((bf16[16,16,448]{1,0,2:T(8,128)(2,1)}), bf16[16,16,7168]{1,0,2:T(8,128)(2,1)}) %all-gather.2.cloned.1.call-update) | async-done | bytes 3670032 | tf_op jit(solution)/shard_map/all_gather | solution.py:44
  236.4 26.5 %copy.36 = bf16[16,16,7168]{2,1,0:T(8,128)(2,1)} copy(bf16[16,16,7168]{1,0,2:T(8,128)(2,1)} %all-gather.2.cloned.1.call-done) | data formatting | bytes 7340032 | tf_op jit(solution)/shard_map/all_gather | solution.py:44
  262.9 7.9 %all-to-all-start.3 = ((bf16[16,16,7168]{2,1,0:T(8,128)(2,1)}), bf16[16,16,7168]{2,1,0:T(8,128)(2,1)}, u32[]{:S(2)}, u32[]{:S(2)}) async-start(bf16[16,16,7168]{2,1,0:T(8,128)(2,1)} %copy.36), calls=%async_computation.4 | async-start | bytes 7340032 | tf_op jit(solution)/shard_map/all_to_all | solution.py:48
  271.0 3.8 fusion.8
  274.8 3.2 fusion.12
  278.0 75.0 %all-to-all-done.3 = bf16[16,16,7168]{2,1,0:T(8,128)(2,1)} async-done(((bf16[16,16,7168]{2,1,0:T(8,128)(2,1)}), bf16[16,16,7168]{2,1,0:T(8,128)(2,1)}, u32[]{:S(2)}, u32[]{:S(2)}) %all-to-all-start.3) | async-done | bytes 3670048 | tf_op jit(solution)/shard_map/all_to_all | solution.py:48
  353.0 3.1 multiply_convert_fusion.1
  356.2 3.1 convolution_convert_fusion
  359.3 2.7 fusion.10
  362.1 2.9 fusion
  366.5 71.1 %reduce-scatter.3.cloned.1.call-done = bf16[256,448]{0,1:T(8,128)(2,1)} async-done(((bf16[256,7168]{0,1:T(8,128)(2,1)}), bf16[256,448]{0,1:T(8,128)(2,1)}) %reduce-scatter.3.cloned.1.call-update) | async-done | bytes 229392 | tf_op jit(solution)/shard_map/reduce_scatter | solution.py:23
  439.4 9.4 %all-to-all-start.2 = ((bf16[16,16,448]{2,1,0:T(8,128)(2,1)}), bf16[16,16,448]{2,1,0:T(8,128)(2,1)S(1)}, u32[]{:S(2)}, u32[]{:S(2)}) async-start(bf16[16,16,448]{2,1,0:T(8,128)(2,1)} %bitcast.8), calls=%async_computation.3 | async-start | bytes 524288 | tf_op jit(solution)/shard_map/all_to_all | solution.py:26
  448.7 4.0 fusion.3
  452.7 70.2 %reduce-scatter.5.cloned.1.call-done = bf16[256,448]{0,1:T(8,128)(2,1)} async-done(((bf16[256,7168]{0,1:T(8,128)(2,1)}), bf16[256,448]{0,1:T(8,128)(2,1)}) %reduce-scatter.5.cloned.1.call-update) | async-done | bytes 229392 | tf_op jit(solution)/shard_map/reduce_scatter | solution.py:23
  524.6 9.4 %all-to-all-start.4 = ((bf16[16,16,448]{2,1,0:T(8,128)(2,1)}), bf16[16,16,448]{2,1,0:T(8,128)(2,1)}, u32[]{:S(2)}, u32[]{:S(2)}) async-start(bf16[16,16,448]{2,1,0:T(8,128)(2,1)} %bitcast.12), calls=%async_computation.6 | async-start | bytes 524288 | tf_op jit(solution)/shard_map/all_to_all | solution.py:26
  534.0 4.4 fusion.2
  538.5 4.4 fusion.1
  546.4 2.8 scatter_custom_fusion.1
  (49 shorter events, 18.8 us)
Async XLA Ops:
  7.2 345.8 %copy-start = (bf16[1,128,7168]{2,1,0:T(8,128)(2,1)S(1)}, bf16[1,128,7168]{2,1,0:T(8,128)(2,1)}, u32[]{:S(2)}) copy-start(bf16[1,128,7168]{2,1,0:T(8,128)(2,1)} %param.14) | copy-start | bytes 5505028
  14.1 8.3 %copy-start.5 = (f32[16,1,16]{2,1,0:T(1,128)S(1)}, f32[16,1,16]{2,1,0:T(1,128)}, u32[]{:S(2)}) copy-start(f32[16,1,16]{2,1,0:T(1,128)} %param.17) | copy-start | bytes 3076
  14.1 9.1 %copy-start.3 = (bf16[512,448]{0,1:T(8,128)(2,1)S(1)}, bf16[512,448]{0,1:T(8,128)(2,1)}, u32[]{:S(2)}) copy-start(bf16[512,448]{0,1:T(8,128)(2,1)} %param.11) | copy-start | bytes 1376260
  14.1 78.2 %all-to-all-start = ((bf16[16,16,16,448]{3,2,1,0:T(8,128)(2,1)}), bf16[16,16,16,448]{3,2,1,0:T(8,128)(2,1)}, u32[]{:S(2)}, u32[]{:S(2)}) async-start(bf16[16,16,16,448]{3,2,1,0:T(8,128)(2,1)} %stack.3), calls=%async_computation | async-start | bytes 8388608 | tf_op jit(solution)/shard_map/all_to_all | solution.py:42
  21.8 214.5 %all-gather.2.cloned.1.call-start = ((), (), s32[]{:S(2)}) async-start(), calls=%async_computation.8 | async-start | bytes 31195136 | tf_op jit(solution)/shard_map/all_gather | solution.py:44
  107.3 155.6 %all-to-all-start.1 = ((bf16[16,16,7168]{2,1,0:T(8,128)(2,1)}), bf16[16,16,7168]{2,1,0:T(8,128)(2,1)}, u32[]{:S(2)}, u32[]{:S(2)}) async-start(bf16[16,16,7168]{2,1,0:T(8,128)(2,1)} %reshape.102), calls=%async_computation.1 | async-start | bytes 7340032 | tf_op jit(solution)/shard_map/all_to_all | solution.py:47
  262.9 90.1 %all-to-all-start.3 = ((bf16[16,16,7168]{2,1,0:T(8,128)(2,1)}), bf16[16,16,7168]{2,1,0:T(8,128)(2,1)}, u32[]{:S(2)}, u32[]{:S(2)}) async-start(bf16[16,16,7168]{2,1,0:T(8,128)(2,1)} %copy.36), calls=%async_computation.4 | async-start | bytes 7340032 | tf_op jit(solution)/shard_map/all_to_all | solution.py:48
  270.7 166.8 %reduce-scatter.3.cloned.1.call-start = ((), (), s32[]{:S(2)}) async-start(), calls=%async_computation.7 | async-start | bytes 3899392 | tf_op jit(solution)/shard_map/reduce_scatter | solution.py:23
  271.0 3.9 copy-start.2
  359.3 163.6 %reduce-scatter.5.cloned.1.call-start = ((), (), s32[]{:S(2)}) async-start(), calls=%async_computation.9 | async-start | bytes 3899392 | tf_op jit(solution)/shard_map/reduce_scatter | solution.py:23
  359.3 2.8 copy-start.1
  365.0 0.7 copy-start.4
  439.4 85.3 %all-to-all-start.2 = ((bf16[16,16,448]{2,1,0:T(8,128)(2,1)}), bf16[16,16,448]{2,1,0:T(8,128)(2,1)S(1)}, u32[]{:S(2)}, u32[]{:S(2)}) async-start(bf16[16,16,448]{2,1,0:T(8,128)(2,1)} %bitcast.8), calls=%async_computation.3 | async-start | bytes 524288 | tf_op jit(solution)/shard_map/all_to_all | solution.py:26
  524.6 21.7 %all-to-all-start.4 = ((bf16[16,16,448]{2,1,0:T(8,128)(2,1)}), bf16[16,16,448]{2,1,0:T(8,128)(2,1)}, u32[]{:S(2)}, u32[]{:S(2)}) async-start(bf16[16,16,448]{2,1,0:T(8,128)(2,1)} %bitcast.12), calls=%async_computation.6 | async-start | bytes 524288 | tf_op jit(solution)/shard_map/all_to_all | solution.py:26
Sparse Core Ops, SparseCore 0:
  26.7 209.5 all-gather.1
  359.4 78.1 reduce-scatter.2
  441.2 81.5 reduce-scatter.4
